TPU v7x, 32 devices: a whole 2x2x4 slice. The times are simulated.
32 devices in a mesh: space: 8 (over z, x), member: 4 (over y, core).
Axes of the slice: x: 2, y: 2, z: 4, core: 2. Of those that a mesh axis runs over, the one named last changes fastest.
Arguments:
- prediction_maps: bfloat16 [4, 72, 16, 1440], P('member', None, 'space'), may hold values from -6 to 6
- truth_analysis: float32 [72, 23040], P(None, ('space', 'member')), may hold values from -6 to 6
- reciprocal_spread: float32 [72], replicated, may hold values from 0.3 to 3
- deconv_inputs: bfloat16 [4, 72, 16, 1440], P('member', None, 'space'), may hold values from -6 to 6
- filter_tensor: bfloat16 [5, 5, 72, 72], replicated, may hold values from -0.125 to 0.125
Outputs:
- grad_hidden: bfloat16 [4, 72, 16, 1440], P('member', None, 'space')
- grad_kernel: float32 [5, 5, 72, 72], replicated
All inputs are finite; a program needn't handle non-finite values.
Results may differ from a plain program's by a relative error of at most 0.018.
Values may be sent and summed in bfloat16 or wider, within the bound.
No kernel may reach another device: no remote copies, remote signals or barrier semaphores. Data moves between devices by JAX's collectives and lax.ppermute only.
A program may use at most 64 MiB of HBM per device.

v0:
```python
import jax
import jax.numpy as jnp
from jax import lax
from jax.sharding import PartitionSpec as P

smoothing = 1.0


def extended(x, sides, width):
    for axis, dim in sides:
        size, length = (lax.axis_size(axis), x.shape[dim])
        up = [(i, (i + 1) % size) for i in range(size - 1)]
        down = [(j, i) for i, j in up]
        last = lax.slice_in_dim(x, length - width, length, axis=dim)
        first = lax.slice_in_dim(x, 0, width, axis=dim)
        before = lax.ppermute(last, axis, up)
        after = lax.ppermute(first, axis, down)
        x = jnp.concatenate([before, x, after], axis=dim)
    return x


def area_weights(rows_total):
    index = jnp.arange(rows_total, dtype=jnp.float32)
    latitude = (index + 0.5) * (jnp.pi / rows_total) - jnp.pi / 2
    cosine = jnp.cos(latitude)
    return cosine / jnp.mean(cosine)


def direct_term(own, target, scale):
    offset = scale * (own - target[None])
    radius = jnp.sqrt(jnp.sum(offset * offset, axis=1, keepdims=True) + smoothing)
    return scale * offset / radius


def pair_sums(scaled_own, scaled_other):
    own_sq = jnp.sum(scaled_own * scaled_own, axis=1)
    other_sq = jnp.sum(scaled_other * scaled_other, axis=1)
    inner = jnp.einsum("mcp,ncp->mnp", scaled_own, scaled_other, precision=lax.Precision.HIGHEST)
    spread_sq = own_sq[:, None, :] + other_sq[None, :, :] - 2.0 * inner + smoothing
    inverse = 1.0 / jnp.sqrt(spread_sq)
    total_weight = jnp.sum(inverse, axis=1)
    mixture = jnp.einsum("mnp,ncp->mcp", inverse, scaled_other, precision=lax.Precision.HIGHEST)
    return (total_weight, mixture)


def body(prediction_maps, truth_analysis, reciprocal_spread, deconv_inputs, filter_tensor):
    quantity_indices = prediction_maps.shape[1]
    parallel_section = prediction_maps.shape[2]
    meridian_extent = prediction_maps.shape[3]
    ksize = filter_tensor.shape[0]
    members = lax.axis_size("member")
    rows_total = parallel_section * lax.axis_size("space")
    pixel_count = parallel_section * meridian_extent
    weights = lax.dynamic_slice_in_dim(
        area_weights(rows_total), lax.axis_index("space") * parallel_section, parallel_section
    )
    scale = reciprocal_spread[None, :, None]
    prediction_vector = prediction_maps.reshape(1, quantity_indices, pixel_count)
    whole_obs = lax.all_gather(truth_analysis, "member", axis=1, tiled=True)
    own = prediction_vector.astype(jnp.float32)
    direct = direct_term(own, whole_obs, scale)
    scaled_own = scale * own
    piece = lax.all_gather(prediction_maps, "member", axis=0, tiled=True)
    other = scale * piece.astype(jnp.float32).reshape(piece.shape[0], quantity_indices, pixel_count)
    weight_part, mix_part = pair_sums(scaled_own, other)
    paired = scale * (scaled_own * weight_part[:, None, :] - mix_part)
    terms = (direct - paired / members).reshape(quantity_indices, parallel_section, meridian_extent)
    grad_out = (terms * weights[None, :, None]).astype(jnp.bfloat16)
    padded = extended(grad_out, (("space", 1),), 2)
    wrapped = jnp.concatenate([padded[:, :, -2:], padded, padded[:, :, :2]], axis=2)
    flat_hidden = deconv_inputs[0].reshape(quantity_indices, pixel_count)
    back = jnp.zeros((quantity_indices, pixel_count), jnp.float32)
    pieces = []
    for row_shift in range(ksize):
        band = wrapped[:, row_shift : row_shift + parallel_section, :]
        stacked = jnp.stack(
            [band[:, :, col_shift : col_shift + meridian_extent] for col_shift in range(ksize)]
        ).reshape(ksize * quantity_indices, pixel_count)
        row_filter = jnp.transpose(filter_tensor[row_shift], (1, 0, 2)).reshape(
            quantity_indices, ksize * quantity_indices
        )
        back = back + jnp.dot(row_filter, stacked, preferred_element_type=jnp.float32)
        product = lax.dot_general(
            flat_hidden, stacked, (((1,), (1,)), ((), ())), preferred_element_type=jnp.float32
        )
        pieces.append(
            jnp.transpose(product.reshape(quantity_indices, ksize, quantity_indices), (1, 0, 2))
        )
    partial_sum = jnp.stack(pieces)
    grad_hidden = back.astype(jnp.bfloat16).reshape(
        1, quantity_indices, parallel_section, meridian_extent
    )
    kernel_total = lax.psum(partial_sum, ("space", "member"))
    norm_factor = 1.0 / jnp.sqrt(jnp.float32(members * rows_total * meridian_extent))
    return (grad_hidden, kernel_total * norm_factor)


def solution(mesh):
    return jax.shard_map(
        body,
        mesh=mesh,
        in_specs=(
            P("member", None, "space", None),
            P(None, ("space", "member")),
            P(),
            P("member", None, "space", None),
            P(),
        ),
        out_specs=(P("member", None, "space", None), P()),
        check_vma=False,
    )
```

profile of v0, /device:TPU:0, one launch (start us, length us, event | category | flops | bytes accessed | tf_op | source)
XLA Modules:
  0.0 303.7 jit_solution(18112935933690532214)
XLA Ops:
  7.2 1.9 copy.52
  10.8 10.8 %all-gather = f32[4,720,72]{1,2,0:T(8,128)S(1)} all-gather(f32[1,720,72]{1,2,0:T(8,128)S(1)} %bitcast.231), channel_id=1, replica_groups=mesh['space'=8,'member'=4] {'member'}, dimensions={0}, use_global_device_ids=true | all-gather | bytes 1036800 | tf_op jit(solution)/shard_map/all_gather | solution.py:59
  25.4 8.2 %all-gather.3.cloned.1.call-done = bf16[4,72,2,1440]{3,1,2,0:T(8,128)(2,1)} async-done(((bf16[1,72,2,1440]{3,1,2,0:T(8,128)(2,1)}), bf16[4,72,2,1440]{3,1,2,0:T(8,128)(2,1)}) %all-gather.3.cloned.1.call-update) | async-done | bytes 1658896 | tf_op jit(solution)/shard_map/all_gather | solution.py:63
  33.6 4.6 %copy.53 = f32[4,72,2,1440]{3,2,1,0:T(2,128)} copy(bf16[4,72,2,1440]{3,1,2,0:T(8,128)(2,1)} %all-gather.3.cloned.1.call-done) | data formatting | bytes 4976640 | tf_op jit(solution)/shard_map/convert_element_type | solution.py:64
  38.2 4.7 %reshape.235 = f32[4,72,2880]{2,1,0:T(8,128)S(1)} reshape(f32[4,72,2,1440]{3,2,1,0:T(2,128)} %copy.53) | data formatting | bytes 6635520 | tf_op jit(solution)/shard_map/reshape | solution.py:64
  42.9 2.1 multiply_reduce_fusion
  45.2 1.6 multiply_reduce_fusion.2
  50.3 3.4 %collective-permute-start = (bf16[72,2,1440]{2,1,0:T(2,128)(2,1)S(1)}, bf16[72,2,1440]{2,1,0:T(2,128)(2,1)S(1)}, u32[]{:S(2)}, u32[]{:S(2)}) collective-permute-start(bf16[72,2,1440]{2,1,0:T(2,128)(2,1)S(1)} %multiply_convert_fusion.1), channel_id=1, source_target_pairs={{0,4},{4,8},{8,12},{12,16},{16,20},{20,24},{24,28},{1,5},{5,9},{9,... | collective-permute-start | bytes 1244168 | tf_op jit(solution)/shard_map/ppermute | solution.py:16
  53.7 1.5 collective-permute-start.1
  60.2 12.7 %collective-permute-done = bf16[72,2,1440]{2,1,0:T(2,128)(2,1)S(1)} collective-permute-done((bf16[72,2,1440]{2,1,0:T(2,128)(2,1)S(1)}, bf16[72,2,1440]{2,1,0:T(2,128)(2,1)S(1)}, u32[]{:S(2)}, u32[]{:S(2)}) %collective-permute-start) | collective-permute-done | bytes 414752 | tf_op jit(solution)/shard_map/ppermute | solution.py:16
  72.9 7.4 %fusion.2 = (bf16[72,6,1442]{2,1,0:T(8,128)(2,1)S(1)}, bf16[72,6,1442]{2,1,0:T(8,128)(2,1)S(1)}) fusion(bf16[72,2,1440]{2,1,0:T(2,128)(2,1)} %collective-permute-done.1, bf16[72,2,1440]{2,1,0:T(2,128)(2,1)S(1)} %multiply_convert_fusion.1, bf16[72,2,1440]{2,1,0:T(2,128)(2,1)S(1)} %collective-permute-done), kind=kLoop, calls=%fused_computation.10 | loop fusion | flops 14950656 | bytes 3735936 | tf_op jit(solution)/shard_map/concatenate | solution.py:70
  80.3 1.6 fusion.12
  82.0 5.2 %fusion.11 = (bf16[5,72,2,1440]{3,2,1,0:T(2,128)(2,1)S(1)}, bf16[5,72,2,1440]{3,2,1,0:T(2,128)(2,1)S(1)}, bf16[5,72,2,1440]{3,2,1,0:T(2,128)(2,1)S(1)}, bf16[5,7...) fusion(bf16[5,72,2,1440]{3,2,1,0:T(2,128)(2,1)S(1)} %get-tuple-element.25, ...), kind=kLoop, calls=%fused_computation.38 | loop fusion | bytes 4423680
  87.6 3.8 %bitcast_dynamic-update-slice_fusion = (bf16[5,72,2,1440]{3,2,1,0:T(2,128)(2,1)S(1)}, bf16[5,72,2,1440]{3,2,1,0:T(2,128)(2,1)S(1)}, bf16[5,72,2,1440]{3,2,1,0:T(2,128)(2,1)S(1)}, bf16[5,72,2,1440]{3,2,1,0:T(2,128)(2,1)S(1)}) fusion(bf16[5,72,2,1440]{3,2,1,0:T(2,128)(2,1)S(1)} %get-tuple-element.20, bf16[72,2,1440]{2,1,0:T(2,128)(2,1)} %collective-permute-done.1, ...), kind=kLoop, calls=%fused_computation.79 | loop fusion | flops 1658880 | bytes 3068928
  91.3 5.2 %fusion.10 = (bf16[5,72,2,1440]{3,2,1,0:T(2,128)(2,1)S(1)}, bf16[5,72,2,1440]{3,2,1,0:T(2,128)(2,1)S(1)}, bf16[5,72,2,1440]{3,2,1,0:T(2,128)(2,1)S(1)}, bf16[5,7...) fusion(bf16[5,72,2,1440]{3,2,1,0:T(2,128)(2,1)S(1)} %get-tuple-element.39, ...), kind=kLoop, calls=%fused_computation.36 | loop fusion | bytes 4423680
  96.5 5.4 %fusion.9 = (bf16[5,72,2,1440]{3,2,1,0:T(2,128)(2,1)S(1)}, bf16[5,72,2,1440]{3,2,1,0:T(2,128)(2,1)S(1)}, bf16[5,72,2,1440]{3,2,1,0:T(2,128)(2,1)S(1)}, bf16[5,72...) fusion(bf16[5,72,2,1440]{3,2,1,0:T(2,128)(2,1)S(1)} %get-tuple-element.15, ...), kind=kLoop, calls=%fused_computation.34 | loop fusion | bytes 4423680 | tf_op jit(solution)/shard_map/stack | solution.py:76
  104.6 1.4 copy-done.13
  106.0 1.4 copy-done.14
  107.5 1.4 copy-done.15
  108.8 5.4 %reshape.238 = bf16[360,2880]{1,0:T(8,128)(2,1)S(1)} reshape(bf16[5,72,2,1440]{3,2,1,0:T(2,128)(2,1)} %copy-done.15) | data formatting | bytes 4147200 | tf_op jit(solution)/shard_map/reshape | solution.py:78
  116.7 6.3 %reshape.240 = bf16[360,2880]{1,0:T(8,128)(2,1)} reshape(bf16[5,72,2,1440]{3,2,1,0:T(2,128)(2,1)} %copy-done.14) | data formatting | bytes 4147200 | tf_op jit(solution)/shard_map/reshape | solution.py:78
  123.0 3.0 convolution_bitcast_fusion.3
  126.0 1.7 copy.60
  127.7 6.3 %reshape.243 = bf16[360,2880]{1,0:T(8,128)(2,1)} reshape(bf16[5,72,2,1440]{3,2,1,0:T(2,128)(2,1)} %copy-done.13) | data formatting | bytes 4147200 | tf_op jit(solution)/shard_map/reshape | solution.py:78
  134.0 3.0 convolution_bitcast_fusion.2
  137.0 1.7 copy.61
  138.7 6.2 %reshape.245 = bf16[360,2880]{1,0:T(8,128)(2,1)} reshape(bf16[5,72,2,1440]{3,2,1,0:T(2,128)(2,1)} %copy-done.12) | data formatting | bytes 4147200 | tf_op jit(solution)/shard_map/reshape | solution.py:78
  144.9 3.0 convolution_bitcast_fusion.1
  148.0 1.7 copy.62
  149.7 6.2 %reshape.247 = bf16[360,2880]{1,0:T(8,128)(2,1)} reshape(bf16[5,72,2,1440]{3,2,1,0:T(2,128)(2,1)} %copy-done.11) | data formatting | bytes 4147200 | tf_op jit(solution)/shard_map/reshape | solution.py:78
  155.9 3.0 convolution_bitcast_fusion
  170.3 124.0 %all-reduce.2.cloned.1.call-done = f32[5,5,72,72]{2,3,1,0:T(8,128)} async-done(((f32[5,5,72,72]{2,3,1,0:T(8,128)}), f32[5,5,72,72]{2,3,1,0:T(8,128)}) %all-reduce.2.cloned.1.call-update) | async-done | bytes 518416 | tf_op jit(solution)/shard_map/psum | solution.py:93
  (95 shorter events, 32.8 us)
Async XLA Ops:
  7.2 3.3 %copy-start.10 = (bf16[1,72,2,1440]{3,2,1,0:T(2,128)(2,1)S(1)}, bf16[1,72,2,1440]{3,2,1,0:T(2,128)(2,1)}, u32[]{:S(2)}) copy-start(bf16[1,72,2,1440]{3,2,1,0:T(2,128)(2,1)} %param.5) | copy-start | bytes 1244164
  7.2 3.6 %copy-start.24 = (f32[72,720]{1,0:T(8,128)S(1)}, f32[72,720]{1,0:T(8,128)}, u32[]{:S(2)}) copy-start(f32[72,720]{1,0:T(8,128)} %param.6) | copy-start | bytes 622084
  7.2 26.4 %all-gather.3.cloned.1.call-start = ((), (), s32[]{:S(2)}) async-start(), calls=%async_computation | async-start | bytes 2211840 | tf_op jit(solution)/shard_map/all_gather | solution.py:63
  9.1 285.2 %all-reduce.2.cloned.1.call-start = ((), (), s32[]{:S(2)}) async-start(), calls=%async_computation.1 | async-start | bytes 1843200 | tf_op jit(solution)/shard_map/psum | solution.py:93
  10.5 13.8 %copy-start.6 = (f32[72,2880]{1,0:T(8,128)}, f32[72,2880]{1,0:T(8,128)S(1)}, u32[]{:S(2)}) copy-start(f32[72,2880]{1,0:T(8,128)S(1)} %reshape.255) | copy-start | bytes 2488324
  10.8 13.3 %copy-start.4 = (f32[1,72,2880]{2,1,0:T(8,128)}, f32[1,72,2880]{2,1,0:T(8,128)S(1)}, u32[]{:S(2)}) copy-start(f32[1,72,2880]{2,1,0:T(8,128)S(1)} %reshape.256) | copy-start | bytes 2488324
  10.8 13.3 %copy-start.25 = (f32[72]{0:T(128)S(1)}, f32[72]{0:T(128)}, u32[]{:S(2)}) copy-start(f32[72]{0:T(128)} %param.7) | copy-start | bytes 868
  22.5 11.1 %copy-start.8 = (f32[2880,72]{0,1:T(8,128)}, f32[2880,72]{0,1:T(8,128)S(1)}, u32[]{:S(2)}) copy-start(f32[2880,72]{0,1:T(8,128)S(1)} %reshape.258) | copy-start | bytes 2488324
  46.9 1.2 copy-start.5
  46.9 1.4 copy-start.7
  46.9 1.6 copy-start.9
  48.9 6.2 %copy-start.18 = (bf16[1,72,2,1440]{3,2,1,0:T(2,128)(2,1)S(1)}, bf16[1,72,2,1440]{3,2,1,0:T(2,128)(2,1)}, u32[]{:S(2)}) copy-start(bf16[1,72,2,1440]{3,2,1,0:T(2,128)(2,1)} %param.8) | copy-start | bytes 1244164
  48.9 6.6 %copy-start.17 = (bf16[5,5,72,72]{3,2,1,0:T(8,128)(2,1)S(1)}, bf16[5,5,72,72]{3,2,1,0:T(8,128)(2,1)}, u32[]{:S(2)}) copy-start(bf16[5,5,72,72]{3,2,1,0:T(8,128)(2,1)} %param.9) | copy-start | bytes 777604
  50.3 22.7 %collective-permute-start = (bf16[72,2,1440]{2,1,0:T(2,128)(2,1)S(1)}, bf16[72,2,1440]{2,1,0:T(2,128)(2,1)S(1)}, u32[]{:S(2)}, u32[]{:S(2)}) collective-permute-start(bf16[72,2,1440]{2,1,0:T(2,128)(2,1)S(1)} %multiply_convert_fusion.1), channel_id=1, source_target_pairs={{0,4},{4,8},{8,12},{12,16},{16,20},{20,24},{24,28},{1,5},{5,9},{9,... | collective-permute-start | bytes 1244168 | tf_op jit(solution)/shard_map/ppermute | solution.py:16
  53.7 19.3 %collective-permute-start.1 = (bf16[72,2,1440]{2,1,0:T(2,128)(2,1)S(1)}, bf16[72,2,1440]{2,1,0:T(2,128)(2,1)}, u32[]{:S(2)}, u32[]{:S(2)}) collective-permute-start(bf16[72,2,1440]{2,1,0:T(2,128)(2,1)S(1)} %multiply_convert_fusion.1), channel_id=1, source_target_pairs={{4,0},{8,4},{12,8},{16,12},{20,16},{24,20},{28,24},{5,1},{9,5},{13... | collective-permute-start | bytes 1244168 | tf_op jit(solution)/shard_map/ppermute | solution.py:17
  101.9 1.4 copy-start.11
  103.2 1.4 copy-start.12
  104.6 1.4 copy-start.13
  106.0 1.4 copy-start.14
  107.5 1.4 copy-start.15
  158.9 4.9 %copy-start.23 = (bf16[72,5,72]{0,2,1:T(8,128)(2,1)S(1)}, bf16[72,5,72]{0,2,1:T(8,128)(2,1)}, u32[]{:S(2)}) copy-start(bf16[72,5,72]{0,2,1:T(8,128)(2,1)} %copy.54) | copy-start | bytes 155524
  162.8 1.6 copy-start.22
  162.8 0.9 copy-start.16
  163.8 1.6 copy-start
  164.4 1.8 copy-start.1
  164.4 1.8 copy-start.21
  165.9 1.7 copy-start.2
  165.9 1.7 copy-start.20
  166.7 1.8 copy-start.3
  166.7 1.8 copy-start.19
Sparse Core Ops, SparseCore 0:
  10.1 23.4 all-gather.2
  163.9 130.3 all-reduce.1
where the time goes:
time: 305 us; the launch traced here: 304 us
  waiting for transfers between devices  145 us (48%)
  local copies, waits for them, and re-layouts  92.3 us (30%)
  other arithmetic  20 us (7%)
  matrix products  15.6 us (5%)
  between operations  15.2 us (5%)
  blocking collectives  10.8 us (4%)
  starting transfers between devices  4.95 us (2%)
    psum x1, waiting for transfers between devices, body(): kernel_total = lax.psum(partial_sum, ('space', 'member'))  124 us
    unnamed x62, local copies, waits for them, and re-layouts  30.9 us
    reshape x5, local copies, waits for them, and re-layouts, body(): stacked = jnp.stack([band[:, :, col_shift:col_shift + meridian_extent] fo...  30.4 us
    dot_general x5, matrix products, body(): lax.dot_general(flat_hidden, stacked, (((1,), (1,)), ((), ())), preferred...  12.9 us
    ppermute x1, waiting for transfers between devices, extended(): before = lax.ppermute(last, axis, up)  12.7 us
    all_gather x1, blocking collectives, body(): whole_obs = lax.all_gather(truth_analysis, 'member', axis=1, tiled=True)  10.8 us
    all_gather x1, waiting for transfers between devices, body(): piece = lax.all_gather(prediction_maps, 'member', axis=0, tiled=True)  8.17 us
    concatenate x1, other arithmetic, body(): jnp.concatenate([padded[:, :, -2:], padded, padded[:, :, :2]], axis=2)  7.37 us
  transfers between devices with their start and end apart: 4, of which 3 were waited for; matrix products, arithmetic and copies ran while one was open for 5% of the time, Pallas kernels for 0%

commit v1 on v0

--- a/solution.py
+++ b/solution.py
@@ -90,7 +90,7 @@
     grad_hidden = back.astype(jnp.bfloat16).reshape(
         1, quantity_indices, parallel_section, meridian_extent
     )
-    kernel_total = lax.psum(partial_sum, ("space", "member"))
+    kernel_total = lax.psum(lax.psum(partial_sum, "member"), "space")
     norm_factor = 1.0 / jnp.sqrt(jnp.float32(members * rows_total * meridian_extent))
     return (grad_hidden, kernel_total * norm_factor)
 

time: 305 us -> 284 us (0.931)
  waiting for transfers between devices: 145 us -> 128 us
    psum x1 -> x2, waiting for transfers between devices: 124 us -> 109 us  [body(): kernel_total = lax.psum(lax.psum(partial_sum, 'member'), 'space')]
    dot_general x5, matrix products: 12.9 us -> 9.61 us  [body(): lax.dot_general(flat_hidden, stacked, (((1,), (1,)), ((), ())), preferred...]
    unnamed x62 -> x60, local copies, waits for them, and re-layouts: 30.9 us -> 30.5 us
  transfers between devices with their start and end apart: 4 -> 5, of which waited for: 3 -> 4; matrix products, arithmetic and copies ran while one was open for 5% -> 6% of each run, Pallas kernels for 0% -> 0%
where the time goes in v1:
time: 284 us; the launch traced here: 283 us
  waiting for transfers between devices  128 us (45%)
  local copies, waits for them, and re-layouts  92.3 us (32%)
  other arithmetic  17.6 us (6%)
  between operations  14.9 us (5%)
  matrix products  14.1 us (5%)
  blocking collectives  10.8 us (4%)
  starting transfers between devices  5.26 us (2%)
    psum x2, waiting for transfers between devices, body(): kernel_total = lax.psum(lax.psum(partial_sum, 'member'), 'space')  109 us
    unnamed x60, local copies, waits for them, and re-layouts  30.5 us
    reshape x5, local copies, waits for them, and re-layouts, body(): stacked = jnp.stack([band[:, :, col_shift:col_shift + meridian_extent] fo...  28.6 us
    all_gather x1, blocking collectives, body(): whole_obs = lax.all_gather(truth_analysis, 'member', axis=1, tiled=True)  10.8 us
    ppermute x1, waiting for transfers between devices, extended(): before = lax.ppermute(last, axis, up)  10.6 us
    dot_general x5, matrix products, body(): lax.dot_general(flat_hidden, stacked, (((1,), (1,)), ((), ())), preferred...  9.61 us
    all_gather x1, waiting for transfers between devices, body(): piece = lax.all_gather(prediction_maps, 'member', axis=0, tiled=True)  8.17 us
    dot_general x5, local copies, waits for them, and re-layouts, body(): lax.dot_general(flat_hidden, stacked, (((1,), (1,)), ((), ())), preferred...  6.95 us
  transfers between devices with their start and end apart: 5, of which 4 were waited for; matrix products, arithmetic and copies ran while one was open for 6% of the time, Pallas kernels for 0%

profile of v1, /device:TPU:0, one launch (start us, length us, event | category | flops | bytes accessed | tf_op | source)
XLA Modules:
  0.0 282.9 jit_solution(16354958120581019397)
XLA Ops:
  7.2 1.9 copy.52
  10.8 10.8 %all-gather = f32[4,720,72]{1,2,0:T(8,128)S(1)} all-gather(f32[1,720,72]{1,2,0:T(8,128)S(1)} %bitcast.231), channel_id=1, replica_groups=mesh['space'=8,'member'=4] {'member'}, dimensions={0}, use_global_device_ids=true | all-gather | bytes 1036800 | tf_op jit(solution)/shard_map/all_gather | solution.py:59
  25.4 8.2 %all-gather.3.cloned.1.call-done = bf16[4,72,2,1440]{3,1,2,0:T(8,128)(2,1)} async-done(((bf16[1,72,2,1440]{3,1,2,0:T(8,128)(2,1)}), bf16[4,72,2,1440]{3,1,2,0:T(8,128)(2,1)}) %all-gather.3.cloned.1.call-update) | async-done | bytes 1658896 | tf_op jit(solution)/shard_map/all_gather | solution.py:63
  33.6 4.6 %copy.53 = f32[4,72,2,1440]{3,2,1,0:T(2,128)} copy(bf16[4,72,2,1440]{3,1,2,0:T(8,128)(2,1)} %all-gather.3.cloned.1.call-done) | data formatting | bytes 4976640 | tf_op jit(solution)/shard_map/convert_element_type | solution.py:64
  38.2 4.7 %reshape.235 = f32[4,72,2880]{2,1,0:T(8,128)S(1)} reshape(f32[4,72,2,1440]{3,2,1,0:T(2,128)} %copy.53) | data formatting | bytes 6635520 | tf_op jit(solution)/shard_map/reshape | solution.py:64
  42.9 2.1 multiply_reduce_fusion
  45.2 1.6 multiply_reduce_fusion.2
  50.3 3.4 %collective-permute-start = (bf16[72,2,1440]{2,1,0:T(2,128)(2,1)S(1)}, bf16[72,2,1440]{2,1,0:T(2,128)(2,1)S(1)}, u32[]{:S(2)}, u32[]{:S(2)}) collective-permute-start(bf16[72,2,1440]{2,1,0:T(2,128)(2,1)S(1)} %multiply_convert_fusion.1), channel_id=1, source_target_pairs={{0,4},{4,8},{8,12},{12,16},{16,20},{20,24},{24,28},{1,5},{5,9},{9,... | collective-permute-start | bytes 1244168 | tf_op jit(solution)/shard_map/ppermute | solution.py:16
  53.7 1.5 collective-permute-start.1
  62.3 10.6 %collective-permute-done = bf16[72,2,1440]{2,1,0:T(2,128)(2,1)S(1)} collective-permute-done((bf16[72,2,1440]{2,1,0:T(2,128)(2,1)S(1)}, bf16[72,2,1440]{2,1,0:T(2,128)(2,1)S(1)}, u32[]{:S(2)}, u32[]{:S(2)}) %collective-permute-start) | collective-permute-done | bytes 414752 | tf_op jit(solution)/shard_map/ppermute | solution.py:16
  72.9 6.1 %fusion.2 = (bf16[72,6,1442]{2,1,0:T(8,128)(2,1)S(1)}, bf16[72,6,1442]{2,1,0:T(8,128)(2,1)S(1)}) fusion(bf16[72,2,1440]{2,1,0:T(2,128)(2,1)S(1)} %collective-permute-done.1, bf16[72,2,1440]{2,1,0:T(2,128)(2,1)S(1)} %multiply_convert_fusion.1, bf16[72,2,1440]{2,1,0:T(2,128)(2,1)S(1)} %collective-permute-done), kind=kLoop, calls=%fused_computation.10 | loop fusion | flops 14950656 | bytes 3735936 | tf_op jit(solution)/shard_map/concatenate | solution.py:70
  79.1 1.6 fusion.12
  80.7 5.2 %fusion.11 = (bf16[5,72,2,1440]{3,2,1,0:T(2,128)(2,1)S(1)}, bf16[5,72,2,1440]{3,2,1,0:T(2,128)(2,1)S(1)}, bf16[5,72,2,1440]{3,2,1,0:T(2,128)(2,1)S(1)}, bf16[5,7...) fusion(bf16[5,72,2,1440]{3,2,1,0:T(2,128)(2,1)S(1)} %get-tuple-element.25, ...), kind=kLoop, calls=%fused_computation.38 | loop fusion | bytes 4423680
  86.3 2.6 bitcast_dynamic-update-slice_fusion
  88.9 5.2 %fusion.10 = (bf16[5,72,2,1440]{3,2,1,0:T(2,128)(2,1)S(1)}, bf16[5,72,2,1440]{3,2,1,0:T(2,128)(2,1)S(1)}, bf16[5,72,2,1440]{3,2,1,0:T(2,128)(2,1)S(1)}, bf16[5,7...) fusion(bf16[5,72,2,1440]{3,2,1,0:T(2,128)(2,1)S(1)} %get-tuple-element.39, ...), kind=kLoop, calls=%fused_computation.36 | loop fusion | bytes 4423680
  94.1 5.4 %fusion.9 = (bf16[5,72,2,1440]{3,2,1,0:T(2,128)(2,1)S(1)}, bf16[5,72,2,1440]{3,2,1,0:T(2,128)(2,1)S(1)}, bf16[5,72,2,1440]{3,2,1,0:T(2,128)(2,1)S(1)}, bf16[5,72...) fusion(bf16[5,72,2,1440]{3,2,1,0:T(2,128)(2,1)S(1)} %get-tuple-element.15, ...), kind=kLoop, calls=%fused_computation.34 | loop fusion | bytes 4423680 | tf_op jit(solution)/shard_map/stack | solution.py:76
  102.2 1.4 copy-done.14
  103.6 1.4 copy-done.15
  106.4 5.4 %reshape.238 = bf16[360,2880]{1,0:T(8,128)(2,1)S(1)} reshape(bf16[5,72,2,1440]{3,2,1,0:T(2,128)(2,1)} %copy-done.16) | data formatting | bytes 4147200 | tf_op jit(solution)/shard_map/reshape | solution.py:78
  114.3 6.3 %reshape.240 = bf16[360,2880]{1,0:T(8,128)(2,1)} reshape(bf16[5,72,2,1440]{3,2,1,0:T(2,128)(2,1)} %copy-done.15) | data formatting | bytes 4147200 | tf_op jit(solution)/shard_map/reshape | solution.py:78
  120.6 3.0 %convolution_bitcast_fusion.3 = f32[72,360]{1,0:T(8,128)} fusion(bf16[360,2880]{1,0:T(8,128)(2,1)} %reshape.240, bf16[72,2880]{1,0:T(8,128)(2,1)S(1)} %reshape_squeeze.3), kind=kOutput, calls=%fused_computation.18 | convolution fusion | flops 149299200 | bytes 2592000 | tf_op jit(solution)/shard_map/dot_general | solution.py:83
  123.6 1.7 copy.60
  125.3 5.4 %reshape.243 = bf16[360,2880]{1,0:T(8,128)(2,1)S(1)} reshape(bf16[5,72,2,1440]{3,2,1,0:T(2,128)(2,1)} %copy-done.14) | data formatting | bytes 4147200 | tf_op jit(solution)/shard_map/reshape | solution.py:78
  130.7 1.4 convolution_bitcast_fusion.2
  132.1 1.7 copy.61
  133.8 5.4 %reshape.245 = bf16[360,2880]{1,0:T(8,128)(2,1)S(1)} reshape(bf16[5,72,2,1440]{3,2,1,0:T(2,128)(2,1)} %copy-done.13) | data formatting | bytes 4147200 | tf_op jit(solution)/shard_map/reshape | solution.py:78
  140.6 1.7 copy.62
  142.3 6.2 %reshape.247 = bf16[360,2880]{1,0:T(8,128)(2,1)} reshape(bf16[5,72,2,1440]{3,2,1,0:T(2,128)(2,1)} %copy-done.12) | data formatting | bytes 4147200 | tf_op jit(solution)/shard_map/reshape | solution.py:78
  148.5 3.0 %convolution_bitcast_fusion = f32[72,360]{1,0:T(8,128)} fusion(bf16[360,2880]{1,0:T(8,128)(2,1)} %reshape.247, bf16[72,2880]{1,0:T(8,128)(2,1)S(1)} %reshape_squeeze.3), kind=kOutput, calls=%fused_computation.15 | convolution fusion | flops 149299200 | bytes 2592000 | tf_op jit(solution)/shard_map/dot_general | solution.py:83
  156.7 2.3 fusion.38
  161.2 31.9 %all-reduce.3.cloned.1.call-done = f32[5,5,72,72]{2,3,1,0:T(8,128)} async-done(((f32[5,5,72,72]{2,3,1,0:T(8,128)}), f32[5,5,72,72]{2,3,1,0:T(8,128)}) %all-reduce.3.cloned.1.call-update) | async-done | bytes 518416 | tf_op jit(solution)/shard_map/psum | solution.py:93
  196.5 77.4 %all-reduce.5.cloned.1.call-done = f32[5,5,72,72]{2,3,1,0:T(8,128)} async-done(((f32[5,5,72,72]{2,3,1,0:T(8,128)}), f32[5,5,72,72]{2,3,1,0:T(8,128)}) %all-reduce.5.cloned.1.call-update) | async-done | bytes 518416 | tf_op jit(solution)/shard_map/psum | solution.py:93
  (96 shorter events, 37.1 us)
Async XLA Ops:
  7.2 3.3 %copy-start.11 = (bf16[1,72,2,1440]{3,2,1,0:T(2,128)(2,1)S(1)}, bf16[1,72,2,1440]{3,2,1,0:T(2,128)(2,1)}, u32[]{:S(2)}) copy-start(bf16[1,72,2,1440]{3,2,1,0:T(2,128)(2,1)} %param.5) | copy-start | bytes 1244164
  7.2 3.6 %copy-start.23 = (f32[72,720]{1,0:T(8,128)S(1)}, f32[72,720]{1,0:T(8,128)}, u32[]{:S(2)}) copy-start(f32[72,720]{1,0:T(8,128)} %param.6) | copy-start | bytes 622084
  7.2 26.4 %all-gather.3.cloned.1.call-start = ((), (), s32[]{:S(2)}) async-start(), calls=%async_computation | async-start | bytes 2211840 | tf_op jit(solution)/shard_map/all_gather | solution.py:63
  9.1 183.9 %all-reduce.3.cloned.1.call-start = ((), (), s32[]{:S(2)}) async-start(), calls=%async_computation.1 | async-start | bytes 1843200 | tf_op jit(solution)/shard_map/psum | solution.py:93
  10.5 13.8 %copy-start.7 = (f32[72,2880]{1,0:T(8,128)}, f32[72,2880]{1,0:T(8,128)S(1)}, u32[]{:S(2)}) copy-start(f32[72,2880]{1,0:T(8,128)S(1)} %reshape.255) | copy-start | bytes 2488324
  10.8 13.3 %copy-start.5 = (f32[1,72,2880]{2,1,0:T(8,128)}, f32[1,72,2880]{2,1,0:T(8,128)S(1)}, u32[]{:S(2)}) copy-start(f32[1,72,2880]{2,1,0:T(8,128)S(1)} %reshape.256) | copy-start | bytes 2488324
  10.8 13.3 %copy-start.24 = (f32[72]{0:T(128)S(1)}, f32[72]{0:T(128)}, u32[]{:S(2)}) copy-start(f32[72]{0:T(128)} %param.7) | copy-start | bytes 868
  22.5 11.1 %copy-start.9 = (f32[2880,72]{0,1:T(8,128)}, f32[2880,72]{0,1:T(8,128)S(1)}, u32[]{:S(2)}) copy-start(f32[2880,72]{0,1:T(8,128)S(1)} %reshape.258) | copy-start | bytes 2488324
  46.9 1.2 copy-start.6
  46.9 1.4 copy-start.8
  46.9 1.6 copy-start.10
  50.3 22.7 %collective-permute-start = (bf16[72,2,1440]{2,1,0:T(2,128)(2,1)S(1)}, bf16[72,2,1440]{2,1,0:T(2,128)(2,1)S(1)}, u32[]{:S(2)}, u32[]{:S(2)}) collective-permute-start(bf16[72,2,1440]{2,1,0:T(2,128)(2,1)S(1)} %multiply_convert_fusion.1), channel_id=1, source_target_pairs={{0,4},{4,8},{8,12},{12,16},{16,20},{20,24},{24,28},{1,5},{5,9},{9,... | collective-permute-start | bytes 1244168 | tf_op jit(solution)/shard_map/ppermute | solution.py:16
  53.7 19.3 %collective-permute-start.1 = (bf16[72,2,1440]{2,1,0:T(2,128)(2,1)S(1)}, bf16[72,2,1440]{2,1,0:T(2,128)(2,1)S(1)}, u32[]{:S(2)}, u32[]{:S(2)}) collective-permute-start(bf16[72,2,1440]{2,1,0:T(2,128)(2,1)S(1)} %multiply_convert_fusion.1), channel_id=1, source_target_pairs={{4,0},{8,4},{12,8},{16,12},{20,16},{24,20},{28,24},{5,1},{9,5},{13... | collective-permute-start | bytes 1244168 | tf_op jit(solution)/shard_map/ppermute | solution.py:17
  99.5 1.4 copy-start.12
  100.8 1.4 copy-start.13
  102.2 1.4 copy-start.14
  103.6 1.4 copy-start.15
  105.0 1.4 copy-start.16
  111.8 8.8 %copy-start.1 = (bf16[360,2880]{1,0:T(8,128)(2,1)}, bf16[360,2880]{1,0:T(8,128)(2,1)S(1)}, u32[]{:S(2)}) copy-start(bf16[360,2880]{1,0:T(8,128)(2,1)S(1)} %reshape.238) | copy-start | bytes 6220804
  130.7 3.1 %copy-start.3 = (bf16[360,2880]{1,0:T(8,128)(2,1)}, bf16[360,2880]{1,0:T(8,128)(2,1)S(1)}, u32[]{:S(2)}) copy-start(bf16[360,2880]{1,0:T(8,128)(2,1)S(1)} %reshape.243) | copy-start | bytes 6220804
  151.5 5.2 %copy-start.22 = (bf16[72,5,72]{0,2,1:T(8,128)(2,1)S(1)}, bf16[72,5,72]{0,2,1:T(8,128)(2,1)}, u32[]{:S(2)}) copy-start(bf16[72,5,72]{0,2,1:T(8,128)(2,1)} %copy.54) | copy-start | bytes 155524
  155.4 3.6 %copy-start.21 = (bf16[72,5,72]{0,2,1:T(8,128)(2,1)S(1)}, bf16[72,5,72]{0,2,1:T(8,128)(2,1)}, u32[]{:S(2)}) copy-start(bf16[72,5,72]{0,2,1:T(8,128)(2,1)} %copy.55) | copy-start | bytes 155524
  155.4 0.9 copy-start.17
  156.4 117.5 %all-reduce.5.cloned.1.call-start = ((), (), s32[]{:S(2)}) async-start(), calls=%async_computation.2 | async-start | bytes 1843200 | tf_op jit(solution)/shard_map/psum | solution.py:93
  156.7 2.3 copy-start.2
  159.0 1.6 copy-start.4
  159.0 1.6 copy-start.20
  160.6 32.4 %copy-start.19 = (bf16[72,5,72]{0,2,1:T(8,128)(2,1)S(1)}, bf16[72,5,72]{0,2,1:T(8,128)(2,1)}, u32[]{:S(2)}) copy-start(bf16[72,5,72]{0,2,1:T(8,128)(2,1)} %copy.57) | copy-start | bytes 155524
  193.0 0.9 copy-start.18
  193.0 1.6 copy-start
Sparse Core Ops, SparseCore 0:
  10.1 23.4 all-gather.2
  156.5 36.4 all-reduce.2
  196.5 77.3 all-reduce.4
